TPU v7x, 768 devices: a whole 4x8x12 slice. The times are simulated.
768 devices in a mesh: cells: 768 (over y, z, x, core).
Axes of the slice: x: 4, y: 8, z: 12, core: 2. Of those that a mesh axis runs over, the one named last changes fastest.
Arguments:
- block: bfloat16 [165888, 128], P('cells'), may hold values from -6 to 6
- cell_matrix: bfloat16 [768, 343, 343], P('cells'), may hold values from -1 to 3
- connectivity: int32 [768, 343], P('cells'), may hold values from 0 to 342, as said below
- potential: float32 [263424], P('cells'), may hold values from -1.5 to 1.5
- locked: bfloat16 [165888, 704], P('cells'), may hold values from -0.015625 to 0.015625
Outputs:
- filtered: bfloat16 [165888, 128], P('cells')
- intersection: float32 [704, 128], replicated
Inputs may be any that keep to these rules, and one draw needn't show every extreme that they name: `connectivity`: A partition's 1 row list each of its 1 x 1 x 1 cells once, in some order; a row gives the local slots of that sixth-order hexahedron's 343 nodes, in some order, where a node with local coordinates (i, j, k), each from 0 to 6, has slot (i * 7 + j) * 7 + k; neighbouring cells share nodes.
All inputs are finite; a program needn't handle non-finite values.
Results may differ from a plain program's by a relative error of at most 0.0067.
Values may be sent and summed in bfloat16 or wider, within the bound.
A program may use at most 32 MiB of HBM per device.

v0:
```python
import jax
import jax.numpy as jnp
from jax import lax
from jax.sharding import PartitionSpec as P

GRID_Y = 4
GRID_Z = 4
SIDE = 7


chebyshev_coeffs = ((-1.0 / 7.0, 0.0), (-7.0 / 41.0, 8.0 / 41.0), (-41.0 / 259.0, 28.0 / 259.0))
centre = 6.0


def passed_along(value, axis, by):
    count = lax.axis_size(axis)
    pairs = [(i, i + by) for i in range(count) if 0 <= i + by < count]
    return lax.ppermute(value, axis, pairs)


def advance(applied, previous, older, coeffs):
    return (
        coeffs[0] * (applied - centre * previous.astype(jnp.float32))
        - coeffs[1] * older.astype(jnp.float32)
    ).astype(jnp.bfloat16)


def set_first(field, plane, axis_dim):
    rest = lax.slice_in_dim(field, 1, field.shape[axis_dim], axis=axis_dim)
    return jnp.concatenate([jnp.expand_dims(plane, axis_dim), rest], axis=axis_dim)


def add_last(field, plane, axis_dim):
    length = field.shape[axis_dim]
    front = lax.slice_in_dim(field, 0, length - 1, axis=axis_dim)
    last_plane = lax.index_in_dim(field, length - 1, axis_dim, keepdims=False) + plane
    return jnp.concatenate([front, jnp.expand_dims(last_plane, axis_dim)], axis=axis_dim)


def per_device(block, cell_matrix, connectivity, potential, locked):
    owned_rows = block.shape[0]
    slot_count = potential.shape[0]
    columns = block.shape[1]
    edge = SIDE - 1
    position = lax.axis_index("cells")
    grid_x = lax.axis_size("cells") // (GRID_Y * GRID_Z)
    coords = (position // (GRID_Y * GRID_Z), position // GRID_Z % GRID_Y, position % GRID_Z)
    counts = (grid_x, GRID_Y, GRID_Z)
    stride = (GRID_Y * GRID_Z, GRID_Z, 1)
    older = block
    current = block
    for coeffs in chebyshev_coeffs:
        field = (
            jnp.zeros((SIDE, SIDE, SIDE, columns), jnp.bfloat16)
            .at[1:, 1:, 1:]
            .set(current.reshape(edge, edge, edge, columns))
        )
        for axis_dim in range(3):
            plane = lax.index_in_dim(field, SIDE - 1, axis_dim, keepdims=False)
            arrived = passed_along(plane, "cells", stride[axis_dim])
            arrived = jnp.where(coords[axis_dim] > 0, arrived, jnp.zeros_like(arrived))
            field = set_first(field, arrived, axis_dim)
        local_rows = field.reshape(slot_count, columns)
        gathered = jnp.take(local_rows, connectivity, axis=0)
        products = jnp.einsum(
            "cij,cjs->cis", cell_matrix, gathered, preferred_element_type=jnp.float32
        )
        summed = (
            jnp.zeros((slot_count, columns), jnp.float32)
            .at[connectivity.reshape(-1)]
            .add(products.reshape(-1, columns))
        )
        partial_value = (summed + potential[:, None] * local_rows.astype(jnp.float32)).reshape(
            SIDE, SIDE, SIDE, columns
        )
        for axis_dim in (2, 1, 0):
            plane = lax.index_in_dim(partial_value, 0, axis_dim, keepdims=False)
            arrived = passed_along(plane, "cells", -stride[axis_dim])
            arrived = jnp.where(coords[axis_dim] < counts[axis_dim] - 1, arrived, 0.0)
            partial_value = add_last(partial_value, arrived, axis_dim)
        following = advance(
            partial_value[1:, 1:, 1:].reshape(owned_rows, columns), current, older, coeffs
        )
        older = current
        current = following
    partial_intersection = jnp.einsum(
        "nl,ns->ls", locked, current, preferred_element_type=jnp.float32
    )
    intersection = lax.psum(partial_intersection, "cells")
    return (current, intersection)


def solution(mesh):
    in_specs = (
        P("cells", None),
        P("cells", None, None),
        P("cells", None),
        P("cells"),
        P("cells", None),
    )
    out_specs = (P("cells", None), P())
    return jax.shard_map(
        per_device, mesh=mesh, in_specs=in_specs, out_specs=out_specs, check_vma=False
    )
```

profile of v0, /device:TPU:1, one launch (start us, length us, event | category | flops | bytes accessed | tf_op | source)
XLA Modules:
  0.0 662.8 jit_solution(3391541922142066908)
XLA Ops:
  8.1 6.6 collective-permute-start
  15.6 4.6 collective-permute-start.1
  21.2 4.5 collective-permute-start.2
  26.7 1.4 gather_fusion
  29.4 2.4 scatter_fusion
  32.0 1.9 collective-permute-start.3
  33.9 3.8 collective-permute-done.3
  39.1 6.4 collective-permute-done.4
  45.6 1.3 collective-permute-start.5
  46.9 10.3 %collective-permute-done.5 = f32[7,7,128]{2,1,0:T(8,128)S(1)} collective-permute-done((f32[7,7,128]{2,1,0:T(8,128)S(1)}, f32[7,7,128]{2,1,0:T(8,128)S(1)}, u32[]{:S(2)}, u32[]{:S(2)}) %collective-permute-start.5) | collective-permute-done | bytes 25120 | tf_op jit(solution)/shard_map/ppermute | solution.py:18
  58.2 6.3 collective-permute-start.6
  65.4 1.6 collective-permute-start.7
  68.0 5.2 collective-permute-start.8
  74.2 1.4 gather_fusion.1
  76.1 2.4 scatter_fusion.1
  78.6 2.1 collective-permute-start.9
  80.7 3.6 collective-permute-done.9
  84.4 1.3 collective-permute-start.10
  85.7 5.9 collective-permute-done.10
  93.0 10.8 %collective-permute-done.11 = f32[7,7,128]{2,1,0:T(8,128)S(1)} collective-permute-done((f32[7,7,128]{2,1,0:T(8,128)S(1)}, f32[7,7,128]{2,1,0:T(8,128)S(1)}, u32[]{:S(2)}, u32[]{:S(2)}) %collective-permute-start.11) | collective-permute-done | bytes 25120 | tf_op jit(solution)/shard_map/ppermute | solution.py:18
  104.0 8.2 %collective-permute-start.12 = (bf16[7,7,128]{2,0,1:T(8,128)(2,1)S(1)}, bf16[7,7,128]{2,0,1:T(8,128)(2,1)S(1)}, u32[]{:S(2)}, u32[]{:S(2)}) collective-permute-start(bf16[7,7,128]{2,0,1:T(8,128)(2,1)S(1)} %fusion.76), channel_id=1, source_target_pairs={{0,16},{1,17},{2,18},{3,19},{4,20},{5,21},{6,22},{7,23},{8,24},{9,... | collective-permute-start | bytes 37640 | tf_op jit(solution)/shard_map/ppermute | solution.py:18
  113.1 1.6 collective-permute-start.13
  115.7 2.7 collective-permute-start.14
  118.5 3.3 collective-permute-done.14
  121.9 1.4 gather_fusion.2
  123.8 2.4 scatter_fusion.2
  126.4 2.1 collective-permute-start.15
  128.4 3.1 collective-permute-done.15
  132.9 6.1 collective-permute-done.16
  140.4 11.2 %collective-permute-done.17 = f32[7,7,128]{2,1,0:T(8,128)S(1)} collective-permute-done((f32[7,7,128]{2,1,0:T(8,128)S(1)}, f32[7,7,128]{2,1,0:T(8,128)S(1)}, u32[]{:S(2)}, u32[]{:S(2)}) %collective-permute-start.17) | collective-permute-done | bytes 25120 | tf_op jit(solution)/shard_map/ppermute | solution.py:18
  152.8 501.5 %all-reduce.5.cloned.1.call-done = f32[704,128]{1,0:T(8,128)} async-done(((f32[704,128]{1,0:T(8,128)}), f32[704,128]{1,0:T(8,128)}) %all-reduce.5.cloned.1.call-update) | async-done | bytes 360464 | tf_op jit(solution)/shard_map/psum | solution.py:89
  654.2 1.7 copy.336
  (126 shorter events, 18.4 us)
Async XLA Ops:
  7.2 144.5 %copy-start = (bf16[216,704]{1,0:T(8,128)(2,1)S(1)}, bf16[216,704]{1,0:T(8,128)(2,1)}, u32[]{:S(2)}) copy-start(bf16[216,704]{1,0:T(8,128)(2,1)} %param.17) | copy-start | bytes 912388
  7.2 647.1 %all-reduce.5.cloned.1.call-start = ((), (), s32[]{:S(2)}) async-start(), calls=%async_computation | async-start | bytes 720896 | tf_op jit(solution)/shard_map/psum | solution.py:89
  8.1 6.7 %copy-start.5 = (s32[1,343]{1,0:T(1,128)S(1)}, s32[1,343]{1,0:T(1,128)}, u32[]{:S(2)}) copy-start(s32[1,343]{1,0:T(1,128)} %param.15) | copy-start | bytes 4120
  8.1 7.5 %collective-permute-start = (bf16[7,7,128]{2,0,1:T(8,128)(2,1)S(1)}, bf16[7,7,128]{2,0,1:T(8,128)(2,1)S(1)}, u32[]{:S(2)}, u32[]{:S(2)}) collective-permute-start(bf16[7,7,128]{2,0,1:T(8,128)(2,1)S(1)} %bitcast.195), channel_id=1, source_target_pairs={{0,16},{1,17},{2,18},{3,19},{4,20},{5,21},{6,22},{7,23},{8,24},{9,... | collective-permute-start | bytes 37640 | tf_op jit(solution)/shard_map/ppermute | solution.py:18
  15.6 5.5 collective-permute-start.1
  21.2 5.3 collective-permute-start.2
  26.7 1.4 copy-start.4
  28.1 1.0 copy-start.1
  32.0 5.7 collective-permute-start.3
  37.8 7.8 %collective-permute-start.4 = (f32[7,7,128]{2,1,0:T(8,128)S(1)}, f32[7,7,128]{2,1,0:T(8,128)S(1)}, u32[]{:S(2)}, u32[]{:S(2)}) collective-permute-start(f32[7,7,128]{2,1,0:T(8,128)S(1)} %fusion.69), channel_id=1, source_target_pairs={{4,0},{5,1},{6,2},{7,3},{8,4},{9,5},{10,6},{11,7},{12,8},{13,9},{1... | collective-permute-start | bytes 75272 | tf_op jit(solution)/shard_map/ppermute | solution.py:18
  45.6 11.6 %collective-permute-start.5 = (f32[7,7,128]{2,1,0:T(8,128)S(1)}, f32[7,7,128]{2,1,0:T(8,128)S(1)}, u32[]{:S(2)}, u32[]{:S(2)}) collective-permute-start(f32[7,7,128]{2,1,0:T(8,128)S(1)} %fusion.68), channel_id=1, source_target_pairs={{16,0},{17,1},{18,2},{19,3},{20,4},{21,5},{22,6},{23,7},{24,8},{25... | collective-permute-start | bytes 75272 | tf_op jit(solution)/shard_map/ppermute | solution.py:18
  57.3 0.8 copy-start.2
  58.2 7.2 %collective-permute-start.6 = (bf16[7,7,128]{2,0,1:T(8,128)(2,1)S(1)}, bf16[7,7,128]{2,0,1:T(8,128)(2,1)S(1)}, u32[]{:S(2)}, u32[]{:S(2)}) collective-permute-start(bf16[7,7,128]{2,0,1:T(8,128)(2,1)S(1)} %fusion.75), channel_id=1, source_target_pairs={{0,16},{1,17},{2,18},{3,19},{4,20},{5,21},{6,22},{7,23},{8,24},{9,... | collective-permute-start | bytes 37640 | tf_op jit(solution)/shard_map/ppermute | solution.py:18
  65.4 2.5 collective-permute-start.7
  68.0 6.1 collective-permute-start.8
  78.6 5.7 collective-permute-start.9
  84.4 7.3 %collective-permute-start.10 = (f32[7,7,128]{2,1,0:T(8,128)S(1)}, f32[7,7,128]{2,1,0:T(8,128)S(1)}, u32[]{:S(2)}, u32[]{:S(2)}) collective-permute-start(f32[7,7,128]{2,1,0:T(8,128)S(1)} %fusion.67), channel_id=1, source_target_pairs={{4,0},{5,1},{6,2},{7,3},{8,4},{9,5},{10,6},{11,7},{12,8},{13,9},{1... | collective-permute-start | bytes 75272 | tf_op jit(solution)/shard_map/ppermute | solution.py:18
  91.7 12.2 %collective-permute-start.11 = (f32[7,7,128]{2,1,0:T(8,128)S(1)}, f32[7,7,128]{2,1,0:T(8,128)S(1)}, u32[]{:S(2)}, u32[]{:S(2)}) collective-permute-start(f32[7,7,128]{2,1,0:T(8,128)S(1)} %fusion.66), channel_id=1, source_target_pairs={{16,0},{17,1},{18,2},{19,3},{20,4},{21,5},{22,6},{23,7},{24,8},{25... | collective-permute-start | bytes 75272 | tf_op jit(solution)/shard_map/ppermute | solution.py:18
  104.0 9.0 %collective-permute-start.12 = (bf16[7,7,128]{2,0,1:T(8,128)(2,1)S(1)}, bf16[7,7,128]{2,0,1:T(8,128)(2,1)S(1)}, u32[]{:S(2)}, u32[]{:S(2)}) collective-permute-start(bf16[7,7,128]{2,0,1:T(8,128)(2,1)S(1)} %fusion.76), channel_id=1, source_target_pairs={{0,16},{1,17},{2,18},{3,19},{4,20},{5,21},{6,22},{7,23},{8,24},{9,... | collective-permute-start | bytes 37640 | tf_op jit(solution)/shard_map/ppermute | solution.py:18
  113.1 2.5 collective-permute-start.13
  115.7 6.1 collective-permute-start.14
  126.4 5.2 collective-permute-start.15
  131.6 7.4 %collective-permute-start.16 = (f32[7,7,128]{2,1,0:T(8,128)S(1)}, f32[7,7,128]{2,1,0:T(8,128)S(1)}, u32[]{:S(2)}, u32[]{:S(2)}) collective-permute-start(f32[7,7,128]{2,1,0:T(8,128)S(1)} %fusion.65), channel_id=1, source_target_pairs={{4,0},{5,1},{6,2},{7,3},{8,4},{9,5},{10,6},{11,7},{12,8},{13,9},{1... | collective-permute-start | bytes 75272 | tf_op jit(solution)/shard_map/ppermute | solution.py:18
  139.0 12.5 %collective-permute-start.17 = (f32[7,7,128]{2,1,0:T(8,128)S(1)}, f32[7,7,128]{2,1,0:T(8,128)S(1)}, u32[]{:S(2)}, u32[]{:S(2)}) collective-permute-start(f32[7,7,128]{2,1,0:T(8,128)S(1)} %fusion.64), channel_id=1, source_target_pairs={{16,0},{17,1},{18,2},{19,3},{20,4},{21,5},{22,6},{23,7},{24,8},{25... | collective-permute-start | bytes 75272 | tf_op jit(solution)/shard_map/ppermute | solution.py:18
  151.7 1.1 copy-start.3
Sparse Core Ops, SparseCore 0:
  152.9 501.2 all-reduce.4
where the time goes:
time: 665 us; the launch traced here: 663 us
  waiting for transfers between devices  572 us (86%)
  starting transfers between devices  55.3 us (8%)
  between operations  14.9 us (2%)
  local copies, waits for them, and re-layouts  9.41 us (1%)
  other arithmetic  8.6 us (1%)
    psum x1, waiting for transfers between devices, per_device(): intersection = lax.psum(partial_intersection, 'cells')  501 us
    ppermute x18, waiting for transfers between devices, passed_along(): return lax.ppermute(value, axis, pairs)  71 us
    ppermute x18, starting transfers between devices, passed_along(): return lax.ppermute(value, axis, pairs)  55.3 us
  transfers between devices with their start and end apart: 19, of which 19 were waited for; matrix products, arithmetic and copies ran while one was open for 0% of the time, Pallas kernels for 0%

commit v1 on v0

v1 whole, which is shorter than its diff:
```python
import itertools

import jax
import jax.numpy as jnp
import numpy as np
from jax import lax
from jax.experimental import pallas as pl
from jax.experimental.pallas import tpu as pltpu
from jax.sharding import PartitionSpec as P

GRID = (48, 4, 4)
SIDE = 7
NPC = 343
NP = 384
OWNED = 216
STATES = 128
LOCKED = 704
LPAD = 768
CENTRE = 6.0
COEFFS = ((-1.0 / 7.0, 0.0), (-7.0 / 41.0, 8.0 / 41.0), (-41.0 / 259.0, 28.0 / 259.0))
F32, BF16, I32 = jnp.float32, jnp.bfloat16, jnp.int32
MESH = pl.DeviceIdType.MESH

RING_G, RING_Z, RING_Y = 8, 12, 8
ROWS_G = LPAD // RING_G
OWNERS = 6
ROWS_Y = ROWS_G // OWNERS


def neighbour_blocks():
    every = [o for o in itertools.product((-1, 0, 1), repeat=3) if any(o)]
    faces_first = sorted(every, key=lambda o: sum(map(abs, o)))
    upper = [o for o in faces_first if min(o) >= 0]
    lower = [o for o in faces_first if max(o) <= 0]
    mixed = [o for o in faces_first if min(o) < 0 < max(o)]
    blocks, start = [], 0
    for offset in upper + lower + mixed:
        size = 64 if sum(map(abs, offset)) == 1 else 16
        blocks.append((offset, start, size))
        start += size
    return blocks, start


BLOCKS, ROWS = neighbour_blocks()
UPPER, LOWER = BLOCKS[:7], BLOCKS[7:14]
HALF = 256


def tables():
    pick = np.zeros((ROWS, NP), np.float32)
    where_to = np.zeros((8, ROWS), np.int32)
    where_to[0] = -1
    for offset, start, size in BLOCKS:
        ranges = [{1: (6,), 0: range(SIDE), -1: (0,)}[c] for c in offset]
        for row, node in enumerate(itertools.product(*ranges)):
            i, j, k = node
            pick[start + row, (i * SIDE + j) * SIDE + k] = 1.0
            i, j, k = (n - 6 * c for n, c in zip(node, offset))
            where_to[0, start + row] = (i * SIDE + j) * SIDE + k
        for c in range(3):
            where_to[1 + c, start : start + size] = offset[c]
    return pick, where_to


PICK, WHERE_TO = tables()


def dot(a, b):
    return jnp.dot(a, b, preferred_element_type=F32)


def dot_nt(a, b):
    return lax.dot_general(a, b, (((1,), (1,)), ((), ())), preferred_element_type=F32)


def one_hot(a, b):
    return jnp.where(a == b, 1.0, 0.0).astype(BF16)


def split(n, by):
    q = jnp.floor((n + 0.5) * (1.0 / by))
    return q, n - q * by


def owned_slot(n):
    i, rest = split(n, 36)
    j, k = split(rest, 6)
    return (i + 1.0) * 49.0 + (j + 1.0) * 7.0 + (k + 1.0)


def fiota(shape, dim):
    return lax.broadcasted_iota(I32, shape, dim).astype(F32)


def kernel(
    block_ref, a_ref, conn_ref, pot_ref, locked_ref, pick_ref, where_ref,
    filt_ref, inter_ref,
    mext, mloc, smat, potp, lpad, lown, llt,
    snd0, rcv0, sndl, rcvl, snd1, rcv1, snd2, rcv2, snd3, rcv3,
    buf1, rc1, tot2, buf2, rc2, rc3, buf4, rc5,
    hs, hr, s1, r1, s2, r2, s3, r3, s4, r4, s5, r5,
):
    me = lax.axis_index("cells")
    pos = (me // 16, (me // 4) % 4, me % 4)
    g = me % 8
    z = (me // 8) % 12
    y = me // 96

    def at(offset):
        px, py, pz = ((p + c + n) % n for p, c, n in zip(pos, offset, GRID))
        return px * 16 + py * 4 + pz

    def at_g(d):
        return me - g + (g + d) % RING_G

    def at_z(d):
        return me + 8 * ((z + d) % RING_Z - z)

    def at_y(d):
        return me + 96 * ((y + d) % RING_Y - y)

    barrier = pltpu.get_barrier_semaphore()
    partners = [at(o) for o, _, _ in BLOCKS]
    partners += [at_g(d) for d in range(1, RING_G)]
    partners += [at_z(d) for d in range(1, RING_Z)]
    partners += [at_y(d) for d in range(1, RING_Y)]
    for partner in partners:
        pl.semaphore_signal(barrier, inc=1, device_id=(partner,), device_id_type=MESH)

    def remote(src, dst, send, recv, device):
        return pltpu.make_async_remote_copy(
            src_ref=src, dst_ref=dst, send_sem=send, recv_sem=recv,
            device_id=(device,), device_id_type=MESH,
        )

    def send_blocks(blocks, base, snd, rcv, at_sem):
        for offset, start, size in blocks[::-1]:
            rows = pl.ds(start - base, size)
            remote(snd.at[rows], rcv.at[rows], hs.at[at_sem], hr.at[at_sem], at(offset)).start()

    def whole(snd, rcv, at_sem):
        return remote(snd, rcv, hs.at[at_sem], hr.at[at_sem], at(BLOCKS[0][0]))

    place = one_hot(fiota((NP, OWNED), 0), owned_slot(fiota((NP, OWNED), 1)))
    y_own = dot(place, block_ref[...])
    pick_up = pick_ref[0:HALF, :]
    snd0[...] = dot(pick_up, y_own.astype(BF16)).astype(BF16)
    lpad[:, LOCKED - 64 : LPAD] = jnp.zeros((OWNED, 128), BF16)
    lpad[:, 0:LOCKED] = locked_ref[...]
    lown[...] = dot(place, lpad[...]).astype(BF16)
    sndl[...] = dot(pick_up, lown[...]).astype(BF16)
    pl.semaphore_wait(barrier, len(partners))
    send_blocks(UPPER, 0, snd0, rcv0, 0)
    send_blocks(UPPER, 0, sndl, rcvl, 1)

    ct = one_hot(lax.broadcasted_iota(I32, (NP, NPC), 0), conn_ref[...])
    rows_in_order = dot(ct, a_ref[...]).astype(BF16)
    potp[...] = jnp.zeros_like(potp)
    potp[0:1, 0:NPC] = pot_ref[...]
    on_diagonal = lax.broadcasted_iota(I32, (NP, NP), 0) == lax.broadcasted_iota(I32, (NP, NP), 1)
    full = dot_nt(rows_in_order, ct) + jnp.where(on_diagonal, potp[0:1, :], 0.0)
    rounded = full.astype(BF16)
    mloc[...] = rounded
    lost = jnp.sum(full - rounded.astype(F32), axis=1, keepdims=True)
    mext[...] = dot(pick_ref[...], mloc[...]).astype(BF16)

    slot = where_ref[0:1, :]
    for c in range(3):
        source = pos[c] - where_ref[1 + c : 2 + c, :]
        slot = jnp.where(source < 0, -1, jnp.where(source >= GRID[c], -1, slot))
    smat[...] = one_hot(lax.broadcasted_iota(I32, (NP, ROWS), 0), slot)

    node = fiota((NP, STATES), 0)
    i, rest = split(node, 49)
    j, k = split(rest, 7)
    inside = jnp.where(node < NPC - 0.5, 1.0, 0.0)
    owned = inside
    for local, p in zip((i, j, k), pos):
        inside = jnp.where(local + (6 * p).astype(F32) < 0.5, 0.0, inside)
        owned = jnp.where(local < 0.5, 0.0, owned)

    whole(snd0, rcv0, 0).wait_recv()
    current = (y_own + dot(smat[:, 0:HALF], rcv0[...])).astype(BF16)
    older = current
    for step, (snd, rcv) in enumerate(((snd1, rcv1), (snd2, rcv2))):
        c, d = COEFFS[step]
        snd[...] = dot(mext[...], current).astype(BF16)
        send_blocks(BLOCKS, 0, snd, rcv, 2 + step)
        here = dot(mloc[...], current) + (lost - CENTRE) * current.astype(F32)
        if step == 0:
            whole(sndl, rcvl, 1).wait_recv()
            local_locked = lown[...].astype(F32) + dot(smat[:, 0:HALF], rcvl[...])
            llt[...] = local_locked.T.astype(BF16)
        whole(snd, rcv, 2 + step).wait_recv()
        applied = here + dot(smat[...], rcv[...])
        following = (inside * (c * applied - d * older.astype(F32))).astype(BF16)
        older = current
        current = following

    c, d = COEFFS[2]
    third, second = current.astype(F32), older.astype(F32)
    here = dot(mloc[...], current) + lost * third
    own_terms = owned * (c * CENTRE * third + d * second)
    share = dot(llt[...], (c * here - own_terms).astype(BF16))
    buf1[...] = share.astype(BF16).reshape(RING_G, ROWS_G, STATES)
    for dist in range(1, RING_G):
        remote(
            buf1.at[(g + dist) % RING_G], rc1.at[dist - 1], s1.at[dist - 1], r1.at[dist - 1], at_g(dist)
        ).start()

    snd3[...] = dot(mext[HALF : 2 * HALF, :], current).astype(BF16)
    send_blocks(LOWER, HALF, snd3, rcv3, 4)

    acc = buf1[g].astype(F32)
    for dist in range(1, RING_G):
        remote(buf1.at[0], rc1.at[dist - 1], s1.at[dist - 1], r1.at[dist - 1], at_g(dist)).wait_recv()
        acc = acc + rc1[dist - 1].astype(F32)
    tot2[...] = acc.reshape(OWNERS, ROWS_Y, STATES)
    buf2[...] = acc.astype(BF16).reshape(OWNERS, ROWS_Y, STATES)

    def copy2(dist):
        to = (y + dist) % RING_Y
        return remote(
            buf2.at[jnp.minimum(to, OWNERS - 1)], rc2.at[dist - 1], s2.at[dist - 1], r2.at[dist - 1], at_y(dist)
        )

    for dist in range(1, RING_Y):
        @pl.when((y + dist) % RING_Y < OWNERS)
        def _():
            copy2(dist).start()

    whole(snd3, rcv3, 4).wait_recv()
    applied = here + dot(smat[:, HALF : 2 * HALF], rcv3[...])
    result = (c * (applied - CENTRE * third) - d * second).astype(BF16)
    take = one_hot(fiota((OWNED, NP), 1), owned_slot(fiota((OWNED, NP), 0)))
    filt_ref[...] = dot(take, result).astype(BF16)

    def copy3(dist):
        return remote(rc3.at[0], rc3.at[dist], s3.at[dist - 1], r3.at[dist - 1], at_z(dist))

    def copy4(dist, back=0):
        row = jnp.minimum((y - back + RING_Y) % RING_Y, OWNERS - 1)
        return remote(buf4.at[row], buf4.at[row], s4.at[dist - 1], r4.at[dist - 1], at_y(dist))

    @pl.when(y < OWNERS)
    def _():
        acc = tot2[jnp.minimum(y, OWNERS - 1)]
        for dist in range(1, RING_Y):
            copy2(dist).wait_recv()
            acc = acc + rc2[dist - 1].astype(F32)
        rc3[0] = acc.astype(BF16)
        for dist in range(1, RING_Z):
            copy3(dist).start()
        for dist in range(1, RING_Z):
            copy3(dist).wait_recv()
        total = rc3[z % RING_Z].astype(F32)
        for row in range(1, RING_Z):
            total = total + rc3[(z - row + RING_Z) % RING_Z].astype(F32)
        buf4[jnp.minimum(y, OWNERS - 1)] = total.astype(BF16)
        for dist in range(1, RING_Y):
            copy4(dist).start()

    for dist in range(1, RING_Y):
        @pl.when((y - dist + RING_Y) % RING_Y < OWNERS)
        def _():
            copy4(dist, dist).wait_recv()

    rc5[g] = buf4[...].reshape(ROWS_G, STATES)

    def copy5(dist, back=0):
        row = (g - back + RING_G) % RING_G
        return remote(rc5.at[row], rc5.at[row], s5.at[dist - 1], r5.at[dist - 1], at_g(dist))

    for dist in range(1, RING_G):
        copy5(dist).start()
    for dist in range(1, RING_G):
        copy5(dist, dist).wait_recv()
    inter_ref[...] = rc5[...].reshape(LPAD, STATES)[0:LOCKED, :]

    whole(snd0, rcv0, 0).wait_send()
    whole(sndl, rcvl, 1).wait_send()
    whole(snd1, rcv1, 2).wait_send()
    whole(snd2, rcv2, 3).wait_send()
    whole(snd3, rcv3, 4).wait_send()
    for dist in range(1, RING_G):
        remote(buf1.at[0], rc1.at[dist - 1], s1.at[dist - 1], r1.at[dist - 1], at_g(dist)).wait_send()
        copy5(dist).wait_send()
    for dist in range(1, RING_Y):
        @pl.when((y + dist) % RING_Y < OWNERS)
        def _():
            copy2(dist).wait_send()

    @pl.when(y < OWNERS)
    def _():
        for dist in range(1, RING_Z):
            copy3(dist).wait_send()
        for dist in range(1, RING_Y):
            copy4(dist).wait_send()


def per_device(block, cell_matrix, connectivity, potential, locked):
    vmem = pl.BlockSpec(memory_space=pltpu.VMEM)
    scratch = [
        ((ROWS, NP), BF16), ((NP, NP), BF16), ((NP, ROWS), BF16), ((8, NP), F32),
        ((OWNED, LPAD), BF16), ((NP, LPAD), BF16), ((LPAD, NP), BF16),
        ((HALF, STATES), BF16), ((HALF, STATES), BF16),
        ((HALF, LPAD), BF16), ((HALF, LPAD), BF16),
        ((ROWS, STATES), BF16), ((ROWS, STATES), BF16),
        ((ROWS, STATES), BF16), ((ROWS, STATES), BF16),
        ((HALF, STATES), BF16), ((HALF, STATES), BF16),
        ((RING_G, ROWS_G, STATES), BF16), ((RING_G - 1, ROWS_G, STATES), BF16),
        ((OWNERS, ROWS_Y, STATES), F32), ((OWNERS, ROWS_Y, STATES), BF16),
        ((RING_Y - 1, ROWS_Y, STATES), BF16), ((RING_Z, ROWS_Y, STATES), BF16),
        ((OWNERS, ROWS_Y, STATES), BF16), ((RING_G, ROWS_G, STATES), BF16),
    ]
    sems = (5, 5, 7, 7, 7, 7, 11, 11, 7, 7, 7, 7)
    filtered, intersection = pl.pallas_call(
        kernel,
        out_shape=(
            jax.ShapeDtypeStruct((OWNED, STATES), BF16),
            jax.ShapeDtypeStruct((LOCKED, STATES), BF16),
        ),
        in_specs=[vmem] * 7,
        out_specs=(vmem, vmem),
        scratch_shapes=[pltpu.VMEM(*s) for s in scratch] + [pltpu.SemaphoreType.DMA((n,)) for n in sems],
        compiler_params=pltpu.CompilerParams(
            collective_id=0, has_side_effects=True, vmem_limit_bytes=48 << 20
        ),
        name="filter",
    )(
        block, cell_matrix.reshape(NPC, NPC), connectivity.reshape(1, NPC), potential.reshape(1, NPC), locked,
        jnp.asarray(PICK, BF16), jnp.asarray(WHERE_TO),
    )
    return filtered, intersection.astype(F32)


def solution(mesh):
    in_specs = (
        P("cells", None),
        P("cells", None, None),
        P("cells", None),
        P("cells"),
        P("cells", None),
    )
    out_specs = (P("cells", None), P())
    return jax.shard_map(
        per_device, mesh=mesh, in_specs=in_specs, out_specs=out_specs, check_vma=False
    )
```

time: 665 us -> 77 us (0.12)
  waiting for transfers between devices: 572 us -> 0 us
  Pallas kernels: 0 us -> 69.4 us
  starting transfers between devices: 55.3 us -> 0 us
  between operations: 14.9 us -> 0.65 us
  other arithmetic: 8.6 us -> 0.76 us
    psum x1 -> x0, waiting for transfers between devices: 501 us -> none  [per_device(): intersection = lax.psum(partial_intersection, 'cells')]
    ppermute x18 -> x0, waiting for transfers between devices: 71 us -> none  [passed_along(): return lax.ppermute(value, axis, pairs)]
    pallas_call x0 -> x1, Pallas kernels: none -> 69.4 us  [per_device(): pl.pallas_call(kernel, out_shape=(jax.ShapeDtypeStruct((OWNED, STATES), B...]
    ppermute x18 -> x0, starting transfers between devices: 55.3 us -> none  [passed_along(): return lax.ppermute(value, axis, pairs)]
    scatter-add x3 -> x0, other arithmetic: 7.32 us -> none  [per_device(): summed = jnp.zeros((slot_count, columns), jnp.float32).at[connectivity.re...]
  transfers between devices with their start and end apart: 19 -> 0, of which waited for: 19 -> 0; matrix products, arithmetic and copies ran while one was open for 0% -> 0% of each run, Pallas kernels for 0% -> 0%
where the time goes in v1:
time: 77 us; the launch traced here: 76.6 us
  Pallas kernels  69.4 us (90%)
  local copies, waits for them, and re-layouts  5.84 us (8%)
    pallas_call x1, Pallas kernels, per_device(): pl.pallas_call(kernel, out_shape=(jax.ShapeDtypeStruct((OWNED, STATES), B...  69.4 us
    unnamed x13, local copies, waits for them, and re-layouts  5.15 us

profile of v1, /device:TPU:1, one launch (start us, length us, event | category | flops | bytes accessed | tf_op | source)
XLA Modules:
  0.0 76.6 jit_solution(5812997368154921374)
XLA Ops:
  0.6 0.0 copy-start.5
  0.6 0.7 reshape.11.pot_ref
  1.3 0.0 copy-done.5
  1.3 0.0 copy-start
  1.3 1.0 %copy-done = bf16[704,384]{1,0:T(8,128)(2,1)S(1)} copy-done((bf16[704,384]{1,0:T(8,128)(2,1)S(1)}, bf16[704,384]{1,0:T(8,128)(2,1)}, u32[]{:S(2)}) %copy-start) | copy-done | bytes 540696
  2.4 0.0 copy-start.1
  2.4 1.0 %copy-done.1 = bf16[216,704]{1,0:T(8,128)(2,1)S(1)} copy-done((bf16[216,704]{1,0:T(8,128)(2,1)S(1)}, bf16[216,704]{1,0:T(8,128)(2,1)}, u32[]{:S(2)}) %copy-start.1) | copy-done | bytes 304152
  3.4 0.0 copy-start.2
  3.4 0.9 %copy-done.2 = bf16[1,343,343]{2,1,0:T(8,128)(2,1)S(1)} copy-done((bf16[1,343,343]{2,1,0:T(8,128)(2,1)S(1)}, bf16[1,343,343]{2,1,0:T(8,128)(2,1)}, u32[]{:S(2)}) %copy-start.2) | copy-done | bytes 235322
  4.3 0.0 copy-start.3
  4.3 0.8 %copy-done.3 = bf16[216,128]{1,0:T(8,128)(2,1)S(1)} copy-done((bf16[216,128]{1,0:T(8,128)(2,1)S(1)}, bf16[216,128]{1,0:T(8,128)(2,1)}, u32[]{:S(2)}) %copy-start.3) | copy-done | bytes 55320
  5.1 0.0 copy-start.4
  5.1 0.7 copy-done.4
  5.9 69.4 %filter.1 = (bf16[216,128]{1,0:T(8,128)(2,1)S(1)}, bf16[704,128]{1,0:T(8,128)(2,1)S(1)}) custom-call(bf16[216,128]{1,0:T(8,128)(2,1)S(1)} %copy-done.3, bf16[343,343]{1,0:T(8,128)(2,1)S(1)} %bitcast.1, s32[1,343]{1,0:T(1,128)S(1)} %copy-done.5, f32[1,343]{1,0:T(1,128)S(1)} %reshape.11.pot_ref, bf16[216,704]{1,0:T(8,128)(2,1)S(1)} %copy-done.1, ...), custom_call_target="tpu_custom_call" | custom-call | tf_op jit(solution)/shard_map/filter/pallas_call | solution.py:317
  75.2 0.8 convert_element_type.3
  76.0 0.6 copy.10
Async XLA Ops:
  0.6 0.7 copy-start.5
  1.3 1.0 %copy-start = (bf16[704,384]{1,0:T(8,128)(2,1)S(1)}, bf16[704,384]{1,0:T(8,128)(2,1)}, u32[]{:S(2)}) copy-start(bf16[704,384]{1,0:T(8,128)(2,1)} %constant.4.clone.pick_ref) | copy-start | bytes 1622020
  2.4 1.0 %copy-start.1 = (bf16[216,704]{1,0:T(8,128)(2,1)S(1)}, bf16[216,704]{1,0:T(8,128)(2,1)}, u32[]{:S(2)}) copy-start(bf16[216,704]{1,0:T(8,128)(2,1)} %locked_ref.1) | copy-start | bytes 912388
  3.4 1.0 %copy-start.2 = (bf16[1,343,343]{2,1,0:T(8,128)(2,1)S(1)}, bf16[1,343,343]{2,1,0:T(8,128)(2,1)}, u32[]{:S(2)}) copy-start(bf16[1,343,343]{2,1,0:T(8,128)(2,1)} %param.8) | copy-start | bytes 705898
  4.3 0.8 %copy-start.3 = (bf16[216,128]{1,0:T(8,128)(2,1)S(1)}, bf16[216,128]{1,0:T(8,128)(2,1)}, u32[]{:S(2)}) copy-start(bf16[216,128]{1,0:T(8,128)(2,1)} %block_ref.1) | copy-start | bytes 165892
  5.1 0.7 copy-start.4
